TPU v7x, 32 devices: a whole 2x2x4 slice. The times are simulated.
32 devices in a mesh: tm: 8 (over z, y), rep: 4 (over x, core).
Axes of the slice: x: 2, y: 2, z: 4, core: 2. Of those that a mesh axis runs over, the one named last changes fastest.
Arguments:
- transitions: float32 [32, 512, 512], P(('rep', 'tm')), parts along dimension 0, may hold values from -1 to 1, as said below
- cond_covs: float32 [32, 512, 512], P(('rep', 'tm')), parts along dimension 0, may hold values from -40 to 40, as said below
- transition_est: float32 [2048, 512], P('rep'), parts along dimension 0, may hold values from -0.25 to 0.25
Outputs:
- cov_blocks: float32 [32, 512, 512], P(('rep', 'tm')), parts along dimension 0
- transition_grad: float32 [2048, 512], P('rep'), parts along dimension 0
There are 4 independent parts, one for each index of `rep`. A program takes and returns all parts, laid end to end along the dimension named above; each array names one. Nothing has to cross between parts.
Inputs may be any that keep to these rules, and one draw needn't show every extreme that they name: `transitions`: every block has spectral norm below one. `cond_covs`: every block is symmetric and positive definite.
All inputs are finite; a program needn't handle non-finite values.
Results may differ from a plain program's by a relative error of at most 0.00017.
Values sent between devices are 32-bit elements; how exact they have to be, the bound alone decides.
A program may use at most 192 MiB of HBM per device.

v0:
```python
import jax
import jax.numpy as jnp
from jax import lax
from jax.sharding import PartitionSpec as P

highest = lax.Precision.HIGHEST


def passed_along(block, axis, distance):
    devices = range(lax.axis_size(axis))
    route = [(i - distance, i) for i in devices if i - distance in devices]
    return lax.ppermute(block, axis, route)


def times_transposed(left, right):
    return lax.dot_general(
        left, right, (((1,), (1,)), ((), ())), precision=highest, preferred_element_type=jnp.float32
    )


def product(left, right):
    return jnp.dot(left, right, precision=highest, preferred_element_type=jnp.float32)


def on_device(transitions, cond_covs, transition_est):
    blocks_here = transitions.shape[0]
    width = transitions.shape[1]
    devices = lax.axis_size("tm")
    total_blocks = blocks_here * devices
    position = lax.axis_index("tm")
    combined_gain = transitions[blocks_here - 1]
    combined_noise = cond_covs[blocks_here - 1]
    empty_block = jnp.zeros((width, width), jnp.float32)

    def advance(turn_number, incoming):
        outgoing = (
            product(combined_gain, times_transposed(incoming, combined_gain)) + combined_noise
        )
        return passed_along(outgoing, "tm", -1)

    covariance = lax.fori_loop(0, devices - 1, advance, empty_block)
    transition = transitions[0]
    previous_step_cross = times_transposed(covariance, transition)
    covariance = product(transition, previous_step_cross) + cond_covs[0]
    collected = [covariance]
    current_entry = jnp.where(position * blocks_here + 0 < total_blocks - 1, 1.0, 0.0).astype(
        jnp.float32
    )
    accumulated = current_entry * (previous_step_cross - product(transition_est, covariance))
    gradient = lax.psum(accumulated, "tm") / (total_blocks - 1)
    cov_blocks = jnp.stack(collected[::-1], axis=0)
    return (cov_blocks, gradient)


def solution(mesh):
    return jax.shard_map(
        on_device,
        mesh=mesh,
        in_specs=(P(("rep", "tm"), None, None), P(("rep", "tm"), None, None), P("rep", None)),
        out_specs=(P(("rep", "tm"), None, None), P("rep", None)),
        check_vma=False,
    )
```

profile of v0, /device:TPU:0, one launch (start us, length us, event | category | flops | bytes accessed | tf_op | source)
XLA Modules:
  0.0 345.2 jit_solution(12036947720468812156)
XLA Ops:
  7.2 2.6 copy.5
  11.1 233.2 %while.10 = (s32[]{:T(128)}, f32[512,512]{0,1:T(8,128)S(1)}, f32[512,512]{1,0:T(8,128)S(1)}, f32[512,512]{0,1:T(8,128)}, s32[]{:T(128)}) while((s32[]{:T(128)}, f32[512,512]{0,1:T(8,128)S(1)}, f32[512,512]{1,0:T(8,128)S(1)}, f32[512,512]{0,1:T(8,128)}, s32[]{:T(128)}) %tuple.29), condition=%wide.region_1.0_spmd, body=%wide.region_0.0_spmd.sunk | while | flops 3221487616 | bytes 15728769 | solution.py:41
  11.1 3.5 %fusion.26 = f32[512,512]{1,0:T(8,128)S(1)} fusion(f32[512,512]{0,1:T(8,128)S(1)} %get-tuple-element.66, f32[512,512]{1,0:T(8,128)S(1)} %get-tuple-element.72), kind=kOutput, calls=%fused_computation.11.clone.1 | convolution fusion | flops 1610612736 | bytes 3145728 | tf_op jit(solution)/shard_map/while/body/eval_jaxpr/dot_general | solution.py:16
  14.6 4.4 %fusion.27 = f32[512,512]{0,1:T(8,128)} fusion(f32[512,512]{0,1:T(8,128)S(1)} %copy-done.2, f32[512,512]{1,0:T(8,128)S(1)} %fusion.26, f32[512,512]{1,0:T(8,128)S(1)} %get-tuple-element.72), kind=kOutput, calls=%fused_computation.1.clone.1 | convolution fusion | flops 1610874880 | bytes 4194304 | tf_op jit(solution)/shard_map/while/body/eval_jaxpr/dot_general | solution.py:22
  19.0 1.3 collective-permute-start
  20.3 27.0 %collective-permute-done = f32[512,512]{0,1:T(8,128)S(1)} collective-permute-done((f32[512,512]{0,1:T(8,128)}, f32[512,512]{0,1:T(8,128)S(1)}, u32[]{:S(2)}, u32[]{:S(2)}) %collective-permute-start) | collective-permute-done | bytes 1048608 | tf_op jit(solution)/shard_map/while/body/eval_jaxpr/ppermute | solution.py:12
  47.3 3.5 %fusion.26 = f32[512,512]{1,0:T(8,128)S(1)} fusion(f32[512,512]{0,1:T(8,128)S(1)} %get-tuple-element.66, f32[512,512]{1,0:T(8,128)S(1)} %get-tuple-element.72), kind=kOutput, calls=%fused_computation.11.clone.1 | convolution fusion | flops 1610612736 | bytes 3145728 | tf_op jit(solution)/shard_map/while/body/eval_jaxpr/dot_general | solution.py:16
  50.7 4.4 %fusion.27 = f32[512,512]{0,1:T(8,128)} fusion(f32[512,512]{0,1:T(8,128)S(1)} %copy-done.2, f32[512,512]{1,0:T(8,128)S(1)} %fusion.26, f32[512,512]{1,0:T(8,128)S(1)} %get-tuple-element.72), kind=kOutput, calls=%fused_computation.1.clone.1 | convolution fusion | flops 1610874880 | bytes 4194304 | tf_op jit(solution)/shard_map/while/body/eval_jaxpr/dot_general | solution.py:22
  55.2 1.3 collective-permute-start
  56.5 25.7 %collective-permute-done = f32[512,512]{0,1:T(8,128)S(1)} collective-permute-done((f32[512,512]{0,1:T(8,128)}, f32[512,512]{0,1:T(8,128)S(1)}, u32[]{:S(2)}, u32[]{:S(2)}) %collective-permute-start) | collective-permute-done | bytes 1048608 | tf_op jit(solution)/shard_map/while/body/eval_jaxpr/ppermute | solution.py:12
  82.2 3.5 %fusion.26 = f32[512,512]{1,0:T(8,128)S(1)} fusion(f32[512,512]{0,1:T(8,128)S(1)} %get-tuple-element.66, f32[512,512]{1,0:T(8,128)S(1)} %get-tuple-element.72), kind=kOutput, calls=%fused_computation.11.clone.1 | convolution fusion | flops 1610612736 | bytes 3145728 | tf_op jit(solution)/shard_map/while/body/eval_jaxpr/dot_general | solution.py:16
  85.7 4.4 %fusion.27 = f32[512,512]{0,1:T(8,128)} fusion(f32[512,512]{0,1:T(8,128)S(1)} %copy-done.2, f32[512,512]{1,0:T(8,128)S(1)} %fusion.26, f32[512,512]{1,0:T(8,128)S(1)} %get-tuple-element.72), kind=kOutput, calls=%fused_computation.1.clone.1 | convolution fusion | flops 1610874880 | bytes 4194304 | tf_op jit(solution)/shard_map/while/body/eval_jaxpr/dot_general | solution.py:22
  90.2 1.3 collective-permute-start
  91.5 24.9 %collective-permute-done = f32[512,512]{0,1:T(8,128)S(1)} collective-permute-done((f32[512,512]{0,1:T(8,128)}, f32[512,512]{0,1:T(8,128)S(1)}, u32[]{:S(2)}, u32[]{:S(2)}) %collective-permute-start) | collective-permute-done | bytes 1048608 | tf_op jit(solution)/shard_map/while/body/eval_jaxpr/ppermute | solution.py:12
  116.3 3.5 %fusion.26 = f32[512,512]{1,0:T(8,128)S(1)} fusion(f32[512,512]{0,1:T(8,128)S(1)} %get-tuple-element.66, f32[512,512]{1,0:T(8,128)S(1)} %get-tuple-element.72), kind=kOutput, calls=%fused_computation.11.clone.1 | convolution fusion | flops 1610612736 | bytes 3145728 | tf_op jit(solution)/shard_map/while/body/eval_jaxpr/dot_general | solution.py:16
  119.8 4.4 %fusion.27 = f32[512,512]{0,1:T(8,128)} fusion(f32[512,512]{0,1:T(8,128)S(1)} %copy-done.2, f32[512,512]{1,0:T(8,128)S(1)} %fusion.26, f32[512,512]{1,0:T(8,128)S(1)} %get-tuple-element.72), kind=kOutput, calls=%fused_computation.1.clone.1 | convolution fusion | flops 1610874880 | bytes 4194304 | tf_op jit(solution)/shard_map/while/body/eval_jaxpr/dot_general | solution.py:22
  125.6 24.0 %collective-permute-done = f32[512,512]{0,1:T(8,128)S(1)} collective-permute-done((f32[512,512]{0,1:T(8,128)}, f32[512,512]{0,1:T(8,128)S(1)}, u32[]{:S(2)}, u32[]{:S(2)}) %collective-permute-start) | collective-permute-done | bytes 1048608 | tf_op jit(solution)/shard_map/while/body/eval_jaxpr/ppermute | solution.py:12
  149.6 3.5 %fusion.26 = f32[512,512]{1,0:T(8,128)S(1)} fusion(f32[512,512]{0,1:T(8,128)S(1)} %get-tuple-element.66, f32[512,512]{1,0:T(8,128)S(1)} %get-tuple-element.72), kind=kOutput, calls=%fused_computation.11.clone.1 | convolution fusion | flops 1610612736 | bytes 3145728 | tf_op jit(solution)/shard_map/while/body/eval_jaxpr/dot_general | solution.py:16
  153.1 4.4 %fusion.27 = f32[512,512]{0,1:T(8,128)} fusion(f32[512,512]{0,1:T(8,128)S(1)} %copy-done.2, f32[512,512]{1,0:T(8,128)S(1)} %fusion.26, f32[512,512]{1,0:T(8,128)S(1)} %get-tuple-element.72), kind=kOutput, calls=%fused_computation.1.clone.1 | convolution fusion | flops 1610874880 | bytes 4194304 | tf_op jit(solution)/shard_map/while/body/eval_jaxpr/dot_general | solution.py:22
  158.8 23.2 %collective-permute-done = f32[512,512]{0,1:T(8,128)S(1)} collective-permute-done((f32[512,512]{0,1:T(8,128)}, f32[512,512]{0,1:T(8,128)S(1)}, u32[]{:S(2)}, u32[]{:S(2)}) %collective-permute-start) | collective-permute-done | bytes 1048608 | tf_op jit(solution)/shard_map/while/body/eval_jaxpr/ppermute | solution.py:12
  182.0 3.5 %fusion.26 = f32[512,512]{1,0:T(8,128)S(1)} fusion(f32[512,512]{0,1:T(8,128)S(1)} %get-tuple-element.66, f32[512,512]{1,0:T(8,128)S(1)} %get-tuple-element.72), kind=kOutput, calls=%fused_computation.11.clone.1 | convolution fusion | flops 1610612736 | bytes 3145728 | tf_op jit(solution)/shard_map/while/body/eval_jaxpr/dot_general | solution.py:16
  185.5 4.4 %fusion.27 = f32[512,512]{0,1:T(8,128)} fusion(f32[512,512]{0,1:T(8,128)S(1)} %copy-done.2, f32[512,512]{1,0:T(8,128)S(1)} %fusion.26, f32[512,512]{1,0:T(8,128)S(1)} %get-tuple-element.72), kind=kOutput, calls=%fused_computation.1.clone.1 | convolution fusion | flops 1610874880 | bytes 4194304 | tf_op jit(solution)/shard_map/while/body/eval_jaxpr/dot_general | solution.py:22
  191.2 22.3 %collective-permute-done = f32[512,512]{0,1:T(8,128)S(1)} collective-permute-done((f32[512,512]{0,1:T(8,128)}, f32[512,512]{0,1:T(8,128)S(1)}, u32[]{:S(2)}, u32[]{:S(2)}) %collective-permute-start) | collective-permute-done | bytes 1048608 | tf_op jit(solution)/shard_map/while/body/eval_jaxpr/ppermute | solution.py:12
  213.6 3.5 %fusion.26 = f32[512,512]{1,0:T(8,128)S(1)} fusion(f32[512,512]{0,1:T(8,128)S(1)} %get-tuple-element.66, f32[512,512]{1,0:T(8,128)S(1)} %get-tuple-element.72), kind=kOutput, calls=%fused_computation.11.clone.1 | convolution fusion | flops 1610612736 | bytes 3145728 | tf_op jit(solution)/shard_map/while/body/eval_jaxpr/dot_general | solution.py:16
  217.1 4.4 %fusion.27 = f32[512,512]{0,1:T(8,128)} fusion(f32[512,512]{0,1:T(8,128)S(1)} %copy-done.2, f32[512,512]{1,0:T(8,128)S(1)} %fusion.26, f32[512,512]{1,0:T(8,128)S(1)} %get-tuple-element.72), kind=kOutput, calls=%fused_computation.1.clone.1 | convolution fusion | flops 1610874880 | bytes 4194304 | tf_op jit(solution)/shard_map/while/body/eval_jaxpr/dot_general | solution.py:22
  222.8 21.5 %collective-permute-done = f32[512,512]{0,1:T(8,128)S(1)} collective-permute-done((f32[512,512]{0,1:T(8,128)}, f32[512,512]{0,1:T(8,128)S(1)}, u32[]{:S(2)}, u32[]{:S(2)}) %collective-permute-start) | collective-permute-done | bytes 1048608 | tf_op jit(solution)/shard_map/while/body/eval_jaxpr/ppermute | solution.py:12
  244.3 3.5 %fusion.5 = f32[512,512]{1,0:T(8,128)S(1)} fusion(f32[512,512]{0,1:T(8,128)S(1)} %get-tuple-element.24, f32[1,512,512]{2,1,0:T(8,128)S(1)} %bitcast.41), kind=kOutput, calls=%fused_computation.9 | convolution fusion | flops 1610612736 | bytes 3145728 | tf_op jit(solution)/shard_map/dot_general | solution.py:16
  248.7 3.5 %fusion.3 = f32[512,512]{0,1:T(8,128)S(1)} fusion(f32[512,512]{1,0:T(8,128)S(1)} %fusion.5, f32[1,512,512]{1,2,0:T(8,128)S(1)} %bitcast.44, f32[1,512,512]{2,1,0:T(8,128)S(1)} %bitcast.42), kind=kOutput, calls=%fused_computation.6 | convolution fusion | flops 1610874880 | bytes 4194304 | tf_op jit(solution)/shard_map/dot_general | solution.py:22
  252.2 4.1 %fusion.2 = f32[512,512]{1,0:T(8,128)} fusion(f32[512,512]{1,0:T(8,128)} %copy-done.4, f32[512,512]{0,1:T(8,128)S(1)} %fusion.3, f32[512,512]{1,0:T(8,128)S(1)} %copy-done, f32[]{:T(128)S(6)} %select_n.4), kind=kOutput, calls=%fused_computation.4 | convolution fusion | flops 1611137024 | bytes 4194308 | tf_op jit(solution)/shard_map/dot_general | solution.py:22
  256.3 1.3 copy.7
  257.6 78.5 %all-reduce.2.cloned.1.call-done = f32[512,512]{1,0:T(8,128)} async-done(((f32[512,512]{1,0:T(8,128)}), f32[512,512]{1,0:T(8,128)}) %all-reduce.2.cloned.1.call-update) | async-done | bytes 1048592 | tf_op jit(solution)/shard_map/psum | solution.py:50
  336.1 2.3 broadcast_multiply_fusion
  (29 shorter events, 7.4 us)
Async XLA Ops:
  7.2 245.0 %copy-start = (f32[512,512]{1,0:T(8,128)S(1)}, f32[512,512]{1,0:T(8,128)}, u32[]{:S(2)}) copy-start(f32[512,512]{1,0:T(8,128)} %param.7) | copy-start | bytes 3145732
  7.2 328.9 %all-reduce.2.cloned.1.call-start = ((), (), s32[]{:S(2)}) async-start(), calls=%async_computation | async-start | bytes 2097152 | tf_op jit(solution)/shard_map/psum | solution.py:50
  9.8 1.2 copy-start.1
  11.1 3.5 %copy-start.2 = (f32[512,512]{0,1:T(8,128)S(1)}, f32[512,512]{0,1:T(8,128)}, u32[]{:S(2)}) copy-start(f32[512,512]{0,1:T(8,128)} %get-tuple-element.73) | copy-start | bytes 3145732 | tf_op jit(solution)/shard_map/while
  19.0 28.3 %collective-permute-start = (f32[512,512]{0,1:T(8,128)}, f32[512,512]{0,1:T(8,128)S(1)}, u32[]{:S(2)}, u32[]{:S(2)}) collective-permute-start(f32[512,512]{0,1:T(8,128)} %fusion.27), channel_id=1, source_target_pairs={{4,0},{8,4},{12,8},{16,12},{20,16},{24,20},{28,24},{5,1},{9,5},{13... | collective-permute-start | bytes 3145736 | tf_op jit(solution)/shard_map/while/body/eval_jaxpr/ppermute | solution.py:12
  47.3 3.5 %copy-start.2 = (f32[512,512]{0,1:T(8,128)S(1)}, f32[512,512]{0,1:T(8,128)}, u32[]{:S(2)}) copy-start(f32[512,512]{0,1:T(8,128)} %get-tuple-element.73) | copy-start | bytes 3145732 | tf_op jit(solution)/shard_map/while
  55.2 27.0 %collective-permute-start = (f32[512,512]{0,1:T(8,128)}, f32[512,512]{0,1:T(8,128)S(1)}, u32[]{:S(2)}, u32[]{:S(2)}) collective-permute-start(f32[512,512]{0,1:T(8,128)} %fusion.27), channel_id=1, source_target_pairs={{4,0},{8,4},{12,8},{16,12},{20,16},{24,20},{28,24},{5,1},{9,5},{13... | collective-permute-start | bytes 3145736 | tf_op jit(solution)/shard_map/while/body/eval_jaxpr/ppermute | solution.py:12
  82.2 3.5 %copy-start.2 = (f32[512,512]{0,1:T(8,128)S(1)}, f32[512,512]{0,1:T(8,128)}, u32[]{:S(2)}) copy-start(f32[512,512]{0,1:T(8,128)} %get-tuple-element.73) | copy-start | bytes 3145732 | tf_op jit(solution)/shard_map/while
  90.2 26.2 %collective-permute-start = (f32[512,512]{0,1:T(8,128)}, f32[512,512]{0,1:T(8,128)S(1)}, u32[]{:S(2)}, u32[]{:S(2)}) collective-permute-start(f32[512,512]{0,1:T(8,128)} %fusion.27), channel_id=1, source_target_pairs={{4,0},{8,4},{12,8},{16,12},{20,16},{24,20},{28,24},{5,1},{9,5},{13... | collective-permute-start | bytes 3145736 | tf_op jit(solution)/shard_map/while/body/eval_jaxpr/ppermute | solution.py:12
  116.3 3.5 %copy-start.2 = (f32[512,512]{0,1:T(8,128)S(1)}, f32[512,512]{0,1:T(8,128)}, u32[]{:S(2)}) copy-start(f32[512,512]{0,1:T(8,128)} %get-tuple-element.73) | copy-start | bytes 3145732 | tf_op jit(solution)/shard_map/while
  124.3 25.3 %collective-permute-start = (f32[512,512]{0,1:T(8,128)}, f32[512,512]{0,1:T(8,128)S(1)}, u32[]{:S(2)}, u32[]{:S(2)}) collective-permute-start(f32[512,512]{0,1:T(8,128)} %fusion.27), channel_id=1, source_target_pairs={{4,0},{8,4},{12,8},{16,12},{20,16},{24,20},{28,24},{5,1},{9,5},{13... | collective-permute-start | bytes 3145736 | tf_op jit(solution)/shard_map/while/body/eval_jaxpr/ppermute | solution.py:12
  149.6 3.5 %copy-start.2 = (f32[512,512]{0,1:T(8,128)S(1)}, f32[512,512]{0,1:T(8,128)}, u32[]{:S(2)}) copy-start(f32[512,512]{0,1:T(8,128)} %get-tuple-element.73) | copy-start | bytes 3145732 | tf_op jit(solution)/shard_map/while
  157.5 24.5 %collective-permute-start = (f32[512,512]{0,1:T(8,128)}, f32[512,512]{0,1:T(8,128)S(1)}, u32[]{:S(2)}, u32[]{:S(2)}) collective-permute-start(f32[512,512]{0,1:T(8,128)} %fusion.27), channel_id=1, source_target_pairs={{4,0},{8,4},{12,8},{16,12},{20,16},{24,20},{28,24},{5,1},{9,5},{13... | collective-permute-start | bytes 3145736 | tf_op jit(solution)/shard_map/while/body/eval_jaxpr/ppermute | solution.py:12
  182.0 3.5 %copy-start.2 = (f32[512,512]{0,1:T(8,128)S(1)}, f32[512,512]{0,1:T(8,128)}, u32[]{:S(2)}) copy-start(f32[512,512]{0,1:T(8,128)} %get-tuple-element.73) | copy-start | bytes 3145732 | tf_op jit(solution)/shard_map/while
  190.0 23.6 %collective-permute-start = (f32[512,512]{0,1:T(8,128)}, f32[512,512]{0,1:T(8,128)S(1)}, u32[]{:S(2)}, u32[]{:S(2)}) collective-permute-start(f32[512,512]{0,1:T(8,128)} %fusion.27), channel_id=1, source_target_pairs={{4,0},{8,4},{12,8},{16,12},{20,16},{24,20},{28,24},{5,1},{9,5},{13... | collective-permute-start | bytes 3145736 | tf_op jit(solution)/shard_map/while/body/eval_jaxpr/ppermute | solution.py:12
  213.6 3.5 %copy-start.2 = (f32[512,512]{0,1:T(8,128)S(1)}, f32[512,512]{0,1:T(8,128)}, u32[]{:S(2)}) copy-start(f32[512,512]{0,1:T(8,128)} %get-tuple-element.73) | copy-start | bytes 3145732 | tf_op jit(solution)/shard_map/while
  221.5 22.8 %collective-permute-start = (f32[512,512]{0,1:T(8,128)}, f32[512,512]{0,1:T(8,128)S(1)}, u32[]{:S(2)}, u32[]{:S(2)}) collective-permute-start(f32[512,512]{0,1:T(8,128)} %fusion.27), channel_id=1, source_target_pairs={{4,0},{8,4},{12,8},{16,12},{20,16},{24,20},{28,24},{5,1},{9,5},{13... | collective-permute-start | bytes 3145736 | tf_op jit(solution)/shard_map/while/body/eval_jaxpr/ppermute | solution.py:12
  244.3 4.5 %copy-start.3 = (f32[512,512]{0,1:T(8,128)S(1)}, f32[512,512]{0,1:T(8,128)}, u32[]{:S(2)}) copy-start(f32[512,512]{0,1:T(8,128)} %get-tuple-element.78) | copy-start | bytes 3145732
  247.7 1.0 copy-start.4
Sparse Core Ops, SparseCore 0:
  256.4 79.6 all-reduce.1
where the time goes:
time: 346 us; the launch traced here: 345 us
  waiting for transfers between devices  247 us (71%)
  matrix products  66.4 us (19%)
  between operations  14.1 us (4%)
  starting transfers between devices  9 us (3%)
  local copies, waits for them, and re-layouts  6.14 us (2%)
    ppermute x7, waiting for transfers between devices, passed_along(): return lax.ppermute(block, axis, route)  169 us
    psum x1, waiting for transfers between devices, on_device(): gradient = lax.psum(accumulated, 'tm') / (total_blocks - 1)  78.5 us
    dot_general x9, matrix products, product(): jnp.dot(left, right, precision=highest, preferred_element_type=jnp.float32)  38.7 us
    dot_general x8, matrix products, times_transposed(): lax.dot_general(left, right, (((1,), (1,)), ((), ())), precision=highest,...  27.8 us
    ppermute x7, starting transfers between devices, passed_along(): return lax.ppermute(block, axis, route)  8.96 us
  transfers between devices with their start and end apart: 8, of which 8 were waited for; matrix products, arithmetic and copies ran while one was open for 0% of the time, Pallas kernels for 0%

commit v1 on v0

--- a/solution.py
+++ b/solution.py
@@ -47,7 +47,7 @@
         jnp.float32
     )
     accumulated = current_entry * (previous_step_cross - product(transition_est, covariance))
-    gradient = lax.psum(accumulated, "tm") / (total_blocks - 1)
+    gradient = jnp.sum(lax.all_gather(accumulated, "tm"), axis=0) / (total_blocks - 1)
     cov_blocks = jnp.stack(collected[::-1], axis=0)
     return (cov_blocks, gradient)
 

time: 346 us -> 413 us (1.19)
  waiting for transfers between devices: 247 us -> 293 us
  matrix products: 66.4 us -> 86 us
    all_gather x0 -> x1, waiting for transfers between devices: none -> 125 us  [on_device(): lax.all_gather(accumulated, 'tm')]
    psum x1 -> x0, waiting for transfers between devices: 78.5 us -> none  [on_device(): gradient = lax.psum(accumulated, 'tm') / (total_blocks - 1)]
    dot_general x9, matrix products: 38.7 us -> 48.5 us  [product(): jnp.dot(left, right, precision=highest, preferred_element_type=jnp.float32)]
    dot_general x8, matrix products: 27.8 us -> 37.6 us  [times_transposed(): lax.dot_general(left, right, (((1,), (1,)), ((), ())), precision=highest,...]
    reduce_sum x0 -> x1, other arithmetic: none -> 4.49 us  [on_device(): jnp.sum(lax.all_gather(accumulated, 'tm'), axis=0) / (total_blocks - 1)]
where the time goes in v1:
time: 413 us; the launch traced here: 412 us
  waiting for transfers between devices  293 us (71%)
  matrix products  86 us (21%)
  between operations  14.1 us (3%)
  starting transfers between devices  9 us (2%)
  other arithmetic  5.57 us (1%)
    ppermute x7, waiting for transfers between devices, passed_along(): return lax.ppermute(block, axis, route)  169 us
    all_gather x1, waiting for transfers between devices, on_device(): lax.all_gather(accumulated, 'tm')  125 us
    dot_general x9, matrix products, product(): jnp.dot(left, right, precision=highest, preferred_element_type=jnp.float32)  48.5 us
    dot_general x8, matrix products, times_transposed(): lax.dot_general(left, right, (((1,), (1,)), ((), ())), precision=highest,...  37.6 us
    ppermute x7, starting transfers between devices, passed_along(): return lax.ppermute(block, axis, route)  8.96 us
  transfers between devices with their start and end apart: 8, of which 8 were waited for; matrix products, arithmetic and copies ran while one was open for 0% of the time, Pallas kernels for 0%

profile of v1, /device:TPU:0, one launch (start us, length us, event | category | flops | bytes accessed | tf_op | source)
XLA Modules:
  0.0 412.1 jit_solution(4834440265160289454)
XLA Ops:
  7.2 1.6 copy.5
  9.0 250.2 %while.10 = (s32[]{:T(128)}, f32[512,512]{0,1:T(8,128)S(1)}, f32[512,512]{1,0:T(8,128)}, f32[512,512]{0,1:T(8,128)S(1)}, s32[]{:T(128)}) while((s32[]{:T(128)}, f32[512,512]{0,1:T(8,128)S(1)}, f32[512,512]{1,0:T(8,128)}, f32[512,512]{0,1:T(8,128)S(1)}, s32[]{:T(128)}) %tuple.29), condition=%wide.region_1.0_spmd, body=%wide.region_0.0_spmd.sunk | while | flops 3221487616 | bytes 11534437 | solution.py:41
  9.0 4.7 %fusion.26 = f32[512,512]{1,0:T(8,128)S(1)} fusion(f32[512,512]{0,1:T(8,128)S(1)} %get-tuple-element.66, f32[512,512]{1,0:T(8,128)} %get-tuple-element.72), kind=kOutput, calls=%fused_computation.11.clone.1 | convolution fusion | flops 1610612736 | bytes 3145728 | tf_op jit(solution)/shard_map/while/body/eval_jaxpr/dot_general | solution.py:16
  13.7 5.7 %fusion.27 = f32[512,512]{0,1:T(8,128)} fusion(f32[512,512]{0,1:T(8,128)S(1)} %get-tuple-element.73, f32[512,512]{1,0:T(8,128)S(1)} %fusion.26, f32[512,512]{1,0:T(8,128)} %get-tuple-element.72), kind=kOutput, calls=%fused_computation.1.clone.1 | convolution fusion | flops 1610874880 | bytes 4194304 | tf_op jit(solution)/shard_map/while/body/eval_jaxpr/dot_general | solution.py:22
  19.4 1.3 collective-permute-start
  20.7 27.0 %collective-permute-done = f32[512,512]{0,1:T(8,128)S(1)} collective-permute-done((f32[512,512]{0,1:T(8,128)}, f32[512,512]{0,1:T(8,128)S(1)}, u32[]{:S(2)}, u32[]{:S(2)}) %collective-permute-start) | collective-permute-done | bytes 1048608 | tf_op jit(solution)/shard_map/while/body/eval_jaxpr/ppermute | solution.py:12
  47.6 4.7 %fusion.26 = f32[512,512]{1,0:T(8,128)S(1)} fusion(f32[512,512]{0,1:T(8,128)S(1)} %get-tuple-element.66, f32[512,512]{1,0:T(8,128)} %get-tuple-element.72), kind=kOutput, calls=%fused_computation.11.clone.1 | convolution fusion | flops 1610612736 | bytes 3145728 | tf_op jit(solution)/shard_map/while/body/eval_jaxpr/dot_general | solution.py:16
  52.3 5.7 %fusion.27 = f32[512,512]{0,1:T(8,128)} fusion(f32[512,512]{0,1:T(8,128)S(1)} %get-tuple-element.73, f32[512,512]{1,0:T(8,128)S(1)} %fusion.26, f32[512,512]{1,0:T(8,128)} %get-tuple-element.72), kind=kOutput, calls=%fused_computation.1.clone.1 | convolution fusion | flops 1610874880 | bytes 4194304 | tf_op jit(solution)/shard_map/while/body/eval_jaxpr/dot_general | solution.py:22
  58.0 1.3 collective-permute-start
  59.3 25.7 %collective-permute-done = f32[512,512]{0,1:T(8,128)S(1)} collective-permute-done((f32[512,512]{0,1:T(8,128)}, f32[512,512]{0,1:T(8,128)S(1)}, u32[]{:S(2)}, u32[]{:S(2)}) %collective-permute-start) | collective-permute-done | bytes 1048608 | tf_op jit(solution)/shard_map/while/body/eval_jaxpr/ppermute | solution.py:12
  85.0 4.7 %fusion.26 = f32[512,512]{1,0:T(8,128)S(1)} fusion(f32[512,512]{0,1:T(8,128)S(1)} %get-tuple-element.66, f32[512,512]{1,0:T(8,128)} %get-tuple-element.72), kind=kOutput, calls=%fused_computation.11.clone.1 | convolution fusion | flops 1610612736 | bytes 3145728 | tf_op jit(solution)/shard_map/while/body/eval_jaxpr/dot_general | solution.py:16
  89.8 5.7 %fusion.27 = f32[512,512]{0,1:T(8,128)} fusion(f32[512,512]{0,1:T(8,128)S(1)} %get-tuple-element.73, f32[512,512]{1,0:T(8,128)S(1)} %fusion.26, f32[512,512]{1,0:T(8,128)} %get-tuple-element.72), kind=kOutput, calls=%fused_computation.1.clone.1 | convolution fusion | flops 1610874880 | bytes 4194304 | tf_op jit(solution)/shard_map/while/body/eval_jaxpr/dot_general | solution.py:22
  95.4 1.3 collective-permute-start
  96.7 24.9 %collective-permute-done = f32[512,512]{0,1:T(8,128)S(1)} collective-permute-done((f32[512,512]{0,1:T(8,128)}, f32[512,512]{0,1:T(8,128)S(1)}, u32[]{:S(2)}, u32[]{:S(2)}) %collective-permute-start) | collective-permute-done | bytes 1048608 | tf_op jit(solution)/shard_map/while/body/eval_jaxpr/ppermute | solution.py:12
  121.6 4.7 %fusion.26 = f32[512,512]{1,0:T(8,128)S(1)} fusion(f32[512,512]{0,1:T(8,128)S(1)} %get-tuple-element.66, f32[512,512]{1,0:T(8,128)} %get-tuple-element.72), kind=kOutput, calls=%fused_computation.11.clone.1 | convolution fusion | flops 1610612736 | bytes 3145728 | tf_op jit(solution)/shard_map/while/body/eval_jaxpr/dot_general | solution.py:16
  126.3 5.7 %fusion.27 = f32[512,512]{0,1:T(8,128)} fusion(f32[512,512]{0,1:T(8,128)S(1)} %get-tuple-element.73, f32[512,512]{1,0:T(8,128)S(1)} %fusion.26, f32[512,512]{1,0:T(8,128)} %get-tuple-element.72), kind=kOutput, calls=%fused_computation.1.clone.1 | convolution fusion | flops 1610874880 | bytes 4194304 | tf_op jit(solution)/shard_map/while/body/eval_jaxpr/dot_general | solution.py:22
  133.3 24.0 %collective-permute-done = f32[512,512]{0,1:T(8,128)S(1)} collective-permute-done((f32[512,512]{0,1:T(8,128)}, f32[512,512]{0,1:T(8,128)S(1)}, u32[]{:S(2)}, u32[]{:S(2)}) %collective-permute-start) | collective-permute-done | bytes 1048608 | tf_op jit(solution)/shard_map/while/body/eval_jaxpr/ppermute | solution.py:12
  157.3 4.7 %fusion.26 = f32[512,512]{1,0:T(8,128)S(1)} fusion(f32[512,512]{0,1:T(8,128)S(1)} %get-tuple-element.66, f32[512,512]{1,0:T(8,128)} %get-tuple-element.72), kind=kOutput, calls=%fused_computation.11.clone.1 | convolution fusion | flops 1610612736 | bytes 3145728 | tf_op jit(solution)/shard_map/while/body/eval_jaxpr/dot_general | solution.py:16
  162.0 5.7 %fusion.27 = f32[512,512]{0,1:T(8,128)} fusion(f32[512,512]{0,1:T(8,128)S(1)} %get-tuple-element.73, f32[512,512]{1,0:T(8,128)S(1)} %fusion.26, f32[512,512]{1,0:T(8,128)} %get-tuple-element.72), kind=kOutput, calls=%fused_computation.1.clone.1 | convolution fusion | flops 1610874880 | bytes 4194304 | tf_op jit(solution)/shard_map/while/body/eval_jaxpr/dot_general | solution.py:22
  169.0 23.2 %collective-permute-done = f32[512,512]{0,1:T(8,128)S(1)} collective-permute-done((f32[512,512]{0,1:T(8,128)}, f32[512,512]{0,1:T(8,128)S(1)}, u32[]{:S(2)}, u32[]{:S(2)}) %collective-permute-start) | collective-permute-done | bytes 1048608 | tf_op jit(solution)/shard_map/while/body/eval_jaxpr/ppermute | solution.py:12
  192.1 4.7 %fusion.26 = f32[512,512]{1,0:T(8,128)S(1)} fusion(f32[512,512]{0,1:T(8,128)S(1)} %get-tuple-element.66, f32[512,512]{1,0:T(8,128)} %get-tuple-element.72), kind=kOutput, calls=%fused_computation.11.clone.1 | convolution fusion | flops 1610612736 | bytes 3145728 | tf_op jit(solution)/shard_map/while/body/eval_jaxpr/dot_general | solution.py:16
  196.8 5.7 %fusion.27 = f32[512,512]{0,1:T(8,128)} fusion(f32[512,512]{0,1:T(8,128)S(1)} %get-tuple-element.73, f32[512,512]{1,0:T(8,128)S(1)} %fusion.26, f32[512,512]{1,0:T(8,128)} %get-tuple-element.72), kind=kOutput, calls=%fused_computation.1.clone.1 | convolution fusion | flops 1610874880 | bytes 4194304 | tf_op jit(solution)/shard_map/while/body/eval_jaxpr/dot_general | solution.py:22
  203.8 22.3 %collective-permute-done = f32[512,512]{0,1:T(8,128)S(1)} collective-permute-done((f32[512,512]{0,1:T(8,128)}, f32[512,512]{0,1:T(8,128)S(1)}, u32[]{:S(2)}, u32[]{:S(2)}) %collective-permute-start) | collective-permute-done | bytes 1048608 | tf_op jit(solution)/shard_map/while/body/eval_jaxpr/ppermute | solution.py:12
  226.1 4.7 %fusion.26 = f32[512,512]{1,0:T(8,128)S(1)} fusion(f32[512,512]{0,1:T(8,128)S(1)} %get-tuple-element.66, f32[512,512]{1,0:T(8,128)} %get-tuple-element.72), kind=kOutput, calls=%fused_computation.11.clone.1 | convolution fusion | flops 1610612736 | bytes 3145728 | tf_op jit(solution)/shard_map/while/body/eval_jaxpr/dot_general | solution.py:16
  230.8 5.7 %fusion.27 = f32[512,512]{0,1:T(8,128)} fusion(f32[512,512]{0,1:T(8,128)S(1)} %get-tuple-element.73, f32[512,512]{1,0:T(8,128)S(1)} %fusion.26, f32[512,512]{1,0:T(8,128)} %get-tuple-element.72), kind=kOutput, calls=%fused_computation.1.clone.1 | convolution fusion | flops 1610874880 | bytes 4194304 | tf_op jit(solution)/shard_map/while/body/eval_jaxpr/dot_general | solution.py:22
  237.8 21.5 %collective-permute-done = f32[512,512]{0,1:T(8,128)S(1)} collective-permute-done((f32[512,512]{0,1:T(8,128)}, f32[512,512]{0,1:T(8,128)S(1)}, u32[]{:S(2)}, u32[]{:S(2)}) %collective-permute-start) | collective-permute-done | bytes 1048608 | tf_op jit(solution)/shard_map/while/body/eval_jaxpr/ppermute | solution.py:12
  259.2 4.7 %fusion.5 = f32[512,512]{1,0:T(8,128)S(1)} fusion(f32[512,512]{0,1:T(8,128)S(1)} %get-tuple-element.24, f32[1,512,512]{2,1,0:T(8,128)} %bitcast.42), kind=kOutput, calls=%fused_computation.9 | convolution fusion | flops 1610612736 | bytes 3145728 | tf_op jit(solution)/shard_map/dot_general | solution.py:16
  264.9 4.7 %fusion.3 = f32[512,512]{0,1:T(8,128)S(1)} fusion(f32[512,512]{1,0:T(8,128)S(1)} %fusion.5, f32[1,512,512]{1,2,0:T(8,128)S(1)} %bitcast.45, f32[1,512,512]{2,1,0:T(8,128)} %bitcast.43), kind=kOutput, calls=%fused_computation.6 | convolution fusion | flops 1610874880 | bytes 4194304 | tf_op jit(solution)/shard_map/dot_general | solution.py:22
  269.6 4.1 fusion.2
  273.7 1.3 copy.7
  275.0 124.7 %all-gather.3.cloned.1.call-done = f32[4096,512]{1,0:T(8,128)} async-done(((f32[512,512]{1,0:T(8,128)}), f32[4096,512]{1,0:T(8,128)}) %all-gather.3.cloned.1.call-update) | async-done | bytes 8388624 | tf_op jit(solution)/shard_map/all_gather | solution.py:50
  399.7 4.5 %reduce_sum.9 = f32[512,512]{1,0:T(8,128)S(1)} reduce(f32[8,512,512]{2,1,0:T(8,128)} %bitcast.47, f32[]{:T(128)} %constant.6.clone.1), dimensions={0}, to_apply=%region_2.3 | reduce | flops 1835008 | bytes 9437188 | tf_op jit(solution)/shard_map/reduce_sum | solution.py:50
  (12 shorter events, 7.3 us)
Async XLA Ops:
  7.2 262.5 %copy-start = (f32[512,512]{1,0:T(8,128)S(1)}, f32[512,512]{1,0:T(8,128)}, u32[]{:S(2)}) copy-start(f32[512,512]{1,0:T(8,128)} %param.7) | copy-start | bytes 3145732
  7.2 392.5 %all-gather.3.cloned.1.call-start = ((), (), s32[]{:S(2)}) async-start(), calls=%async_computation | async-start | bytes 9437184 | tf_op jit(solution)/shard_map/all_gather | solution.py:50
  19.4 28.3 %collective-permute-start = (f32[512,512]{0,1:T(8,128)}, f32[512,512]{0,1:T(8,128)S(1)}, u32[]{:S(2)}, u32[]{:S(2)}) collective-permute-start(f32[512,512]{0,1:T(8,128)} %fusion.27), channel_id=1, source_target_pairs={{4,0},{8,4},{12,8},{16,12},{20,16},{24,20},{28,24},{5,1},{9,5},{13... | collective-permute-start | bytes 3145736 | tf_op jit(solution)/shard_map/while/body/eval_jaxpr/ppermute | solution.py:12
  58.0 27.0 %collective-permute-start = (f32[512,512]{0,1:T(8,128)}, f32[512,512]{0,1:T(8,128)S(1)}, u32[]{:S(2)}, u32[]{:S(2)}) collective-permute-start(f32[512,512]{0,1:T(8,128)} %fusion.27), channel_id=1, source_target_pairs={{4,0},{8,4},{12,8},{16,12},{20,16},{24,20},{28,24},{5,1},{9,5},{13... | collective-permute-start | bytes 3145736 | tf_op jit(solution)/shard_map/while/body/eval_jaxpr/ppermute | solution.py:12
  95.4 26.2 %collective-permute-start = (f32[512,512]{0,1:T(8,128)}, f32[512,512]{0,1:T(8,128)S(1)}, u32[]{:S(2)}, u32[]{:S(2)}) collective-permute-start(f32[512,512]{0,1:T(8,128)} %fusion.27), channel_id=1, source_target_pairs={{4,0},{8,4},{12,8},{16,12},{20,16},{24,20},{28,24},{5,1},{9,5},{13... | collective-permute-start | bytes 3145736 | tf_op jit(solution)/shard_map/while/body/eval_jaxpr/ppermute | solution.py:12
  132.0 25.3 %collective-permute-start = (f32[512,512]{0,1:T(8,128)}, f32[512,512]{0,1:T(8,128)S(1)}, u32[]{:S(2)}, u32[]{:S(2)}) collective-permute-start(f32[512,512]{0,1:T(8,128)} %fusion.27), channel_id=1, source_target_pairs={{4,0},{8,4},{12,8},{16,12},{20,16},{24,20},{28,24},{5,1},{9,5},{13... | collective-permute-start | bytes 3145736 | tf_op jit(solution)/shard_map/while/body/eval_jaxpr/ppermute | solution.py:12
  167.7 24.5 %collective-permute-start = (f32[512,512]{0,1:T(8,128)}, f32[512,512]{0,1:T(8,128)S(1)}, u32[]{:S(2)}, u32[]{:S(2)}) collective-permute-start(f32[512,512]{0,1:T(8,128)} %fusion.27), channel_id=1, source_target_pairs={{4,0},{8,4},{12,8},{16,12},{20,16},{24,20},{28,24},{5,1},{9,5},{13... | collective-permute-start | bytes 3145736 | tf_op jit(solution)/shard_map/while/body/eval_jaxpr/ppermute | solution.py:12
  202.5 23.6 %collective-permute-start = (f32[512,512]{0,1:T(8,128)}, f32[512,512]{0,1:T(8,128)S(1)}, u32[]{:S(2)}, u32[]{:S(2)}) collective-permute-start(f32[512,512]{0,1:T(8,128)} %fusion.27), channel_id=1, source_target_pairs={{4,0},{8,4},{12,8},{16,12},{20,16},{24,20},{28,24},{5,1},{9,5},{13... | collective-permute-start | bytes 3145736 | tf_op jit(solution)/shard_map/while/body/eval_jaxpr/ppermute | solution.py:12
  236.5 22.7 %collective-permute-start = (f32[512,512]{0,1:T(8,128)}, f32[512,512]{0,1:T(8,128)S(1)}, u32[]{:S(2)}, u32[]{:S(2)}) collective-permute-start(f32[512,512]{0,1:T(8,128)} %fusion.27), channel_id=1, source_target_pairs={{4,0},{8,4},{12,8},{16,12},{20,16},{24,20},{28,24},{5,1},{9,5},{13... | collective-permute-start | bytes 3145736 | tf_op jit(solution)/shard_map/while/body/eval_jaxpr/ppermute | solution.py:12
  263.9 1.0 copy-start.1
Sparse Core Ops, SparseCore 0:
  273.8 125.8 all-gather.2
